TPU v7x, 128 devices: a whole 4x4x4 slice. The times are simulated.
128 devices in a mesh: section: 8 (over z, x_lo), tp: 16 (over y, x_hi, core).
Axes of the slice: x: 4 (x_hi: 2, x_lo: 2; x = x_hi * 2 + x_lo), y: 4, z: 4, core: 2. Of those that a mesh axis runs over, the one named last changes fastest.
Arguments:
- teacher_rows: bfloat16 [8, 256, 8192], P('section', 'tp'), may hold values from -72 to 72
- norm_gain: float32 [8, 8192], P('section'), may hold values from 0.1 to 1.9
- query_weight: bfloat16 [8, 8192, 8192], P('section', None, 'tp'), may hold values from -2.762136 to 2.762136
- keys_values: bfloat16 [8, 2, 8192, 1024], P('section', None, None, 'tp'), may hold values from -0.071815532 to 0.071815532
- output_weight: bfloat16 [8, 8192, 8192], P('section', 'tp'), may hold values from -0.5 to 0.5
- doc_start: int32 [8], P('section'), may hold values from 1 to 255
- student_rows: bfloat16 [8, 256, 4096], P('section', 'tp'), may hold values from -30 to 30
- projector: bfloat16 [4096, 8192], P('tp', 'section'), may hold values from -1 to 2
Outputs:
- teacher_next: bfloat16 [8, 256, 8192], P('section', 'tp')
- distill_loss: float32 [], replicated
- grad_student: float32 [8, 256, 4096], P('section', 'tp')
- grad_projector: float32 [4096, 8192], P('tp', 'section')
All inputs are finite; a program needn't handle non-finite values.
Results may differ from a plain program's by a relative error of at most 0.02.
Values may be sent and summed in bfloat16 or wider, within the bound.
No kernel may reach another device: no remote copies, remote signals or barrier semaphores. Data moves between devices by JAX's collectives and lax.ppermute only.
A program may use at most 128 MiB of HBM per device.

v0:
```python
import math
import jax
import jax.numpy as jnp
from jax import lax
from jax.sharding import PartitionSpec as P

HD = 128
LOSS_WEIGHT = 64.0
NORM_EPS = 1e-05
COS_EPS = 1e-06


def partner(value, axis, apart):
    mask = 2**apart
    pairs = [(source, source ^ mask) for source in range(lax.axis_size(axis))]
    return lax.ppermute(value, axis, pairs)


def from_everyone(value, axis):
    copies = jnp.broadcast_to(value, (lax.axis_size(axis), *value.shape))
    return lax.all_to_all(copies, axis, split_axis=0, concat_axis=0, tiled=True)


def laid_out(pieces, dim):
    pieces = jnp.moveaxis(pieces, 0, dim)
    shape = pieces.shape
    return pieces.reshape(*shape[:dim], shape[dim] * shape[dim + 1], *shape[dim + 2 :])


def collect(value, axis, dim):
    pieces = from_everyone(value, axis)
    return laid_out(pieces, dim)


def taken_together(value, axis):
    everything = from_everyone(value, axis)
    return jnp.sum(everything, axis=0)


def packed_total(arrays, axis):
    ends = [0]
    for a in arrays:
        ends.append(ends[-1] + a.size)
    subtotal = taken_together(jnp.concatenate([a.ravel() for a in arrays]), axis)
    return tuple((subtotal[b:e].reshape(a.shape) for a, b, e in zip(arrays, ends, ends[1:])))


def cut_along(value, dim, length):
    shape = value.shape
    pieces = value.reshape(*shape[:dim], length, shape[dim] // length, *shape[dim + 1 :])
    return jnp.moveaxis(pieces, dim, 0)


def sent_and_summed(value, axis, dim):
    pieces = cut_along(value, dim, lax.axis_size(axis))
    arrived = lax.all_to_all(pieces, axis, split_axis=0, concat_axis=0, tiled=True)
    return arrived.astype(jnp.float32).sum(axis=0)


def round_bf16(values):
    return lax.optimization_barrier(values.astype(jnp.bfloat16)).astype(jnp.float32)


def join_halves(mine, other, low_side):
    return jnp.where(
        low_side, jnp.concatenate([mine, other], axis=1), jnp.concatenate([other, mine], axis=1)
    )


def cosine_step(inner, own_sq, target_sq, student_proj, target):
    inv_own = lax.rsqrt(own_sq + COS_EPS)
    inv_target = lax.rsqrt(target_sq + COS_EPS)
    cosine = inner * inv_own * inv_target
    slope = LOSS_WEIGHT * (
        (inner * inv_target * inv_own * inv_own * inv_own)[:, None] * student_proj
        - target * (inv_own * inv_target)[:, None]
    )
    return (cosine, slope.astype(jnp.bfloat16))


def attend(queries, keys_full, values_full, first_new):
    row_total = queries.shape[0]
    kv_heads = keys_full.shape[1] // HD
    group = queries.shape[1] // HD // kv_heads
    query_heads = queries.reshape(row_total, kv_heads, group, HD)
    key_heads = keys_full.reshape(row_total, kv_heads, HD)
    value_heads = values_full.reshape(row_total, kv_heads, HD)
    scale = 1.0 / math.sqrt(HD)
    scores = (
        jnp.einsum("qegd,ked->egqk", query_heads, key_heads, preferred_element_type=jnp.float32)
        * scale
    )
    positions = jnp.arange(row_total, dtype=jnp.int32)
    after_start = positions >= first_new
    visible = (positions[None, :] <= positions[:, None]) & (
        after_start[None, :] == after_start[:, None]
    )
    scores = jnp.where(visible, scores, -1e30)
    row_max = jnp.max(scores, axis=-1, keepdims=True)
    expo = jnp.where(visible, jnp.exp(scores - row_max), 0.0)
    weights = (expo / jnp.sum(expo, axis=-1, keepdims=True)).astype(jnp.bfloat16)
    mixed = jnp.einsum("egqk,ked->qegd", weights, value_heads, preferred_element_type=jnp.float32)
    return mixed.astype(jnp.bfloat16).reshape(row_total, queries.shape[1])


def shards(
    teacher_rows,
    norm_gain,
    query_weight,
    keys_values,
    output_weight,
    doc_start,
    student_rows,
    projector,
):
    span_rows = teacher_rows[0]
    tp_count = lax.axis_size("tp")
    tp_position = lax.axis_index("tp")
    rows_float = span_rows.astype(jnp.float32)
    mean_square = jnp.mean(rows_float * rows_float, axis=1, keepdims=True)
    normed = (rows_float * lax.rsqrt(mean_square + NORM_EPS) * norm_gain[0][None, :]).astype(
        jnp.bfloat16
    )
    query_local = query_weight[0]
    key_local = keys_values[0, 0]
    value_local = keys_values[0, 1]
    query_cols = query_local.shape[1]
    key_cols = key_local.shape[1]
    block_rows = lax.all_gather(normed, "tp", axis=0, tiled=True)
    query_part = jnp.dot(block_rows, query_local, preferred_element_type=jnp.float32).astype(
        jnp.bfloat16
    )
    key_part = jnp.dot(block_rows, key_local, preferred_element_type=jnp.float32).astype(
        jnp.bfloat16
    )
    value_part = jnp.dot(block_rows, value_local, preferred_element_type=jnp.float32).astype(
        jnp.bfloat16
    )
    projected = jnp.concatenate([query_part, key_part, value_part], axis=1)
    queries = projected[:, :query_cols]
    keys_full = projected[:, query_cols : query_cols + key_cols]
    values_full = projected[:, query_cols + key_cols :]
    other_key, other_value = partner((keys_full, values_full), "tp", 0)
    low_side = tp_position // 2**0 % 2 == 0
    keys_full = join_halves(keys_full, other_key, low_side)
    values_full = join_halves(values_full, other_value, low_side)
    mixed_heads = attend(queries, keys_full, values_full, doc_start[0])
    out_local = output_weight[0]
    block = mixed_heads
    attn_sum = lax.psum_scatter(
        round_bf16(jnp.dot(block, out_local, preferred_element_type=jnp.float32)).astype(
            jnp.bfloat16
        ),
        "tp",
        scatter_dimension=0,
        tiled=True,
    ).astype(jnp.float32)
    teacher_next = (rows_float + attn_sum).astype(jnp.bfloat16)
    contract_last = (((1,), (1,)), ((), ()))
    contract_pair = (((0, 1), (0, 1)), ((), ()))
    gathered = collect(student_rows, "section", 0)
    token_count = gathered.shape[0] * gathered.shape[1]
    token_rows = gathered.reshape(token_count, gathered.shape[2])
    arrived = lax.all_to_all(teacher_next[None], "section", split_axis=2, concat_axis=0, tiled=True)
    target = arrived.reshape(token_count, arrived.shape[2]).astype(jnp.float32)
    proj_block = lax.all_gather(projector, "tp", axis=0, tiled=True)
    student_proj = jnp.dot(token_rows, proj_block, preferred_element_type=jnp.float32)
    inner, own_sq, target_sq = packed_total(
        (
            jnp.sum(student_proj * target, axis=1),
            jnp.sum(student_proj * student_proj, axis=1),
            jnp.sum(target * target, axis=1),
        ),
        "section",
    )
    cosine, slope = cosine_step(inner, own_sq, target_sq, student_proj, target)
    loss_total = taken_together(jnp.sum(1.0 - cosine), "tp")
    distill_loss = loss_total / (token_count * tp_count)
    block = slope
    grad_local = sent_and_summed(
        lax.dot_general(
            block, proj_block, contract_last, preferred_element_type=jnp.float32
        ).astype(jnp.bfloat16),
        "section",
        0,
    )
    by_column = lax.all_to_all(gathered, "tp", split_axis=2, concat_axis=1, tiled=True)
    slope_stacked = slope.reshape(gathered.shape[0], gathered.shape[1], slope.shape[1])
    block = by_column
    grad_proj = lax.dot_general(
        block,
        lax.all_gather(slope_stacked, "tp", axis=1, tiled=True),
        contract_pair,
        preferred_element_type=jnp.float32,
    )
    return (teacher_next[None], distill_loss, grad_local[None], grad_proj)


def solution(mesh):
    placed = (
        P("section", "tp", None),
        P("section", None),
        P("section", None, "tp"),
        P("section", None, None, "tp"),
        P("section", "tp", None),
        P("section"),
        P("section", "tp", None),
        P("tp", "section"),
    )
    return jax.shard_map(
        shards,
        mesh=mesh,
        in_specs=placed,
        out_specs=(P("section", "tp", None), P(), P("section", "tp", None), P("tp", "section")),
        check_vma=False,
    )
```

profile of v0, /device:TPU:1, one launch (start us, length us, event | category | flops | bytes accessed | tf_op | source)
XLA Modules:
  0.0 376.0 jit_solution(13403994111314197012)
XLA Ops:
  7.2 1.3 fusion.16
  8.5 1.8 fusion.18
  10.3 0.0 reduce-scatter.2.cloned.1.call-start
  11.0 0.1 fusion.29
  11.2 58.2 %all-gather.4.cloned.1.call-done = bf16[256,8192]{1,0:T(8,128)(2,1)} async-done(((bf16[16,8192]{1,0:T(8,128)(2,1)}), bf16[256,8192]{1,0:T(8,128)(2,1)}) %all-gather.4.cloned.1.call-update) | async-done | bytes 4194320 | tf_op jit(solution)/shard_map/all_gather | solution.py:129
  69.4 4.0 %convolution_convert_fusion.3 = bf16[256,64]{0,1:T(8,128)(2,1)S(1)} fusion(bf16[256,8192]{1,0:T(8,128)(2,1)} %all-gather.4.cloned.1.call-done, bf16[1,2,8192,64]{2,3,1,0:T(8,128)(2,1)} %param.11), kind=kOutput, calls=%fused_computation.13 | convolution fusion | flops 268451840 | bytes 5275648 | tf_op jit(solution)/shard_map/dot_general | solution.py:133
  73.4 0.3 collective-permute-start.1
  73.8 1.4 convolution_convert_fusion.4
  75.2 0.3 collective-permute-start
  75.5 5.8 %fusion.8 = bf16[32,4,8,128]{3,2,1,0:T(8,128)(2,1)S(1)} fusion(bf16[256,8192]{1,0:T(8,128)(2,1)S(1)} %copy-done, bf16[1,8192,512]{2,1,0:T(8,128)(2,1)} %param.10), kind=kOutput, calls=%fused_computation.12 | convolution fusion | flops 2147614720 | bytes 12845056 | tf_op jit(solution)/shard_map/dot_general | solution.py:130
  81.4 0.4 fusion.50
  81.7 0.2 fusion.15
  81.9 0.4 convolution_convert_fusion.2
  82.4 4.5 %convolution_convert_fusion = bf16[256,8192]{1,0:T(8,128)(2,1)} fusion(bf16[256,512]{0,1:T(8,128)(2,1)S(1)} %bitcast.115, bf16[1,512,8192]{2,1,0:T(8,128)(2,1)S(1)} %bitcast.111), kind=kOutput, calls=%fused_computation | convolution fusion | flops 2149580800 | bytes 12845056 | tf_op jit(solution)/shard_map/dot_general | solution.py:151
  86.9 0.2 all-gather.6.cloned.1.call-start
  87.1 0.5 all-gather.6.cloned.1.call-update
  87.6 76.1 %reduce-scatter.2.cloned.1.call-done = bf16[16,8192]{1,0:T(8,128)(2,1)} async-done(((bf16[256,8192]{1,0:T(8,128)(2,1)}), bf16[16,8192]{1,0:T(8,128)(2,1)}) %reduce-scatter.2.cloned.1.call-update) | async-done | bytes 262160 | tf_op jit(solution)/shard_map/reduce_scatter | solution.py:150
  163.7 1.0 fusion.26
  164.7 6.8 %copy.48 = bf16[1,16,8192]{1,0,2:T(2,128)(2,1)} copy(bf16[1,16,8192]{2,1,0:T(8,128)(2,1)S(1)} %fusion.26) | data formatting | bytes 524288 | tf_op jit(solution)/shard_map/broadcast_in_dim | solution.py:196
  171.5 0.5 broadcast.68
  172.0 45.2 %reduce.8 = bf16[8192,16]{1,0:T(8,128)(2,1)S(1)} reduce(bf16[8192,1,16]{2,1,0:T(2,128)(2,1)} %bitcast.106, bf16[]{:T(256)} %broadcast.68), dimensions={1}, to_apply=%bitcast.82.reduce_sub_computation | reduce | bytes 524290
  217.3 2.2 reshape.123
  219.5 10.6 %all_to_all.49 = bf16[8,2,8192]{2,1,0:T(2,128)(2,1)S(1)} all-to-all(bf16[8,2,8192]{2,1,0:T(2,128)(2,1)S(1)} %reshape.123), channel_id=1, replica_groups=mesh['section'=8,'tp'=16] {'section'}, dimensions={0} | all-to-all | bytes 524288 | tf_op jit(solution)/shard_map/all_to_all | solution.py:164
  230.1 1.1 broadcast_in_dim.41
  231.2 3.6 all-to-all-start
  234.8 5.1 %reshape.124 = bf16[8192,1,16]{2,1,0:T(2,128)(2,1)} reshape(bf16[8,2,8192]{2,1,0:T(2,128)(2,1)S(1)} %all_to_all.49) | data formatting | bytes 524288
  239.9 8.5 %convert_multiply_fusion.2 = f32[1,16,8192]{1,0,2:T(1,128)} fusion(bf16[8192,1,16]{2,1,0:T(2,128)(2,1)} %reshape.124), kind=kLoop, calls=%fused_computation.68 | loop fusion | flops 262144 | bytes 786432 | tf_op jit(solution)/shard_map/mul | solution.py:172
  248.4 2.5 reduce_sum.89
  250.8 0.1 reduce_sum.91
  250.9 8.5 %bitcast_convert_fusion = f32[1,16,8192]{1,0,2:T(1,128)} fusion(bf16[8192,1,16]{2,1,0:T(2,128)(2,1)} %reshape.124), kind=kLoop, calls=%fused_computation.72 | loop fusion | flops 131072 | bytes 786432 | tf_op jit(solution)/shard_map/convert_element_type | solution.py:165
  259.4 2.8 copy.49
  262.2 4.7 %fusion.20 = (f32[128]{0:T(128)S(1)}, f32[128]{0:T(128)S(1)}, f32[128,1024]{1,0:T(8,128)S(1)}) fusion(f32[1,16,8,1024]{3,1,2,0:T(8,128)S(1)} %copy.49, bf16[128,4096]{1,0:T(8,128)(2,1)S(1)} %bitcast.108, bf16[4096,1024]{1,0:T(8,128)(2,1)} %all-gather.6.cloned.1.call-done), kind=kOutput, calls=%fused_computation.31 | convolution fusion | flops 1074265856 | bytes 10486784 | tf_op jit(solution)/shard_map/dot_general | solution.py:167
  267.0 9.9 %all_to_all.50 = f32[8,1,384]{2,1,0:T(1,128)S(1)} all-to-all(f32[8,1,384]{2,1,0:T(1,128)S(1)} %broadcast_in_dim.42), channel_id=1, replica_groups=mesh['section'=8,'tp'=16] {'section'}, dimensions={0} | all-to-all | bytes 24576 | tf_op jit(solution)/shard_map/all_to_all | solution.py:21
  276.9 0.6 multiply_multiply_fusion
  277.5 0.8 fusion.23
  278.3 7.3 %copy.54 = bf16[8,16,4096]{1,0,2:T(8,128)(2,1)} copy(bf16[8,16,4096]{2,1,0:T(8,128)(2,1)S(1)} %bitcast.109) | data formatting | bytes 2097152 | tf_op jit(solution)/shard_map/reshape | solution.py:27
  285.7 10.5 %reshape.125 = bf16[16,2,16384]{2,1,0:T(2,128)(2,1)S(1)} reshape(bf16[4096,8,16]{2,1,0:T(8,128)(2,1)} %bitcast.103) | data formatting | bytes 2097152
  296.2 31.7 %all_to_all.51 = bf16[16,2,16384]{2,1,0:T(2,128)(2,1)S(1)} all-to-all(bf16[16,2,16384]{2,1,0:T(2,128)(2,1)S(1)} %reshape.125), channel_id=1, replica_groups=mesh['section'=8,'tp'=16] {'tp'}, dimensions={0} | all-to-all | bytes 2097152 | tf_op jit(solution)/shard_map/all_to_all | solution.py:187
  327.8 1.2 broadcast_in_dim.43
  329.1 5.7 %all-to-all-start.3 = ((f32[16,1,1]{2,1,0:T(1,128)}), f32[16,1,1]{2,1,0:T(1,128)S(1)}, u32[]{:S(2)}, u32[]{:S(2)}) async-start(f32[16,1,1]{2,1,0:T(1,128)} %broadcast_in_dim.43), calls=%async_computation.4 | async-start | bytes 16384 | tf_op jit(solution)/shard_map/all_to_all | solution.py:21
  334.8 7.2 %convolution_convert_fusion.1 = bf16[128,4096]{1,0:T(8,128)(2,1)} fusion(bf16[128,1024]{1,0:T(8,128)(2,1)S(1)} %copy-done.2, bf16[4096,1024]{1,0:T(8,128)(2,1)} %all-gather.6.cloned.1.call-done), kind=kOutput, calls=%fused_computation.4 | convolution fusion | flops 1074266112 | bytes 9699328 | tf_op jit(solution)/shard_map/dot_general | solution.py:181
  342.0 3.6 all-to-all-start.4
  345.6 7.5 %reshape.126 = bf16[4096,8,16]{2,1,0:T(8,128)(2,1)} reshape(bf16[16,2,16384]{2,1,0:T(2,128)(2,1)S(1)} %all_to_all.51) | data formatting | bytes 2097152
  353.1 8.3 %copy.56 = bf16[8,16,16,256]{3,2,1,0:T(8,128)(2,1)S(1)} copy(bf16[8,16,16,256]{2,0,3,1:T(8,128)(2,1)} %bitcast.104) | data formatting | bytes 2097152 | tf_op jit(solution)/shard_map/all_to_all | solution.py:187
  361.4 0.6 reduce_sum.94
  362.7 0.8 convert_reduce_fusion
  363.5 3.5 convolution_bitcast_fusion
  367.0 1.3 copy.57
  (34 shorter events, 0.3 us)
Async XLA Ops:
  7.2 66.6 %copy-start.3 = (bf16[1,2,8192,64]{2,3,1,0:T(8,128)(2,1)S(1)}, bf16[1,2,8192,64]{2,3,1,0:T(8,128)(2,1)}, u32[]{:S(2)}) copy-start(bf16[1,2,8192,64]{2,3,1,0:T(8,128)(2,1)} %param.11) | copy-start | bytes 6291460
  7.2 62.2 %all-gather.4.cloned.1.call-start = ((), (), s32[]{:S(2)}) async-start(), calls=%async_computation.7 | async-start | bytes 4456448 | tf_op jit(solution)/shard_map/all_gather | solution.py:129
  10.3 153.4 %reduce-scatter.2.cloned.1.call-start = ((), (), s32[]{:S(2)}) async-start(), calls=%async_computation.8 | async-start | bytes 4456448 | tf_op jit(solution)/shard_map/reduce_scatter | solution.py:150
  69.4 4.4 %copy-start = (bf16[256,8192]{1,0:T(8,128)(2,1)S(1)}, bf16[256,8192]{1,0:T(8,128)(2,1)}, u32[]{:S(2)}) copy-start(bf16[256,8192]{1,0:T(8,128)(2,1)} %all-gather.4.cloned.1.call-done) | copy-start | bytes 12582916
  73.4 7.9 %collective-permute-start.1 = (bf16[256,64]{0,1:T(8,128)(2,1)S(1)}, bf16[256,64]{0,1:T(8,128)(2,1)S(1)}, u32[]{:S(2)}, u32[]{:S(2)}) collective-permute-start(bf16[256,64]{0,1:T(8,128)(2,1)S(1)} %convolution_convert_fusion.3), channel_id=1, source_target_pairs={{0,1},{1,0},{2,3},{3,2},{4,5},{5,4},{6,7},{7,6},{8,9},{9,8},{10,11... | collective-permute-start | bytes 98312 | tf_op jit(solution)/shard_map/ppermute | solution.py:16
  73.8 8.6 %slice-start = ((s8[8388608]{0:T(1024)(128)(4,1)}), s8[4194304]{0:T(1024)(128)(4,1)S(1)}, s32[]{:S(2)}) async-start(s8[8388608]{0:T(1024)(128)(4,1)} %bitcast.110), calls=%async_computation.11 | async-start | bytes 8388608
  75.2 7.2 %slice-start.1 = ((s8[8388608]{0:T(1024)(128)(4,1)}), s8[4194304]{0:T(1024)(128)(4,1)S(1)}, s32[]{:S(2)}) async-start(s8[8388608]{0:T(1024)(128)(4,1)} %bitcast.110), calls=%async_computation.12 | async-start | bytes 8388608
  75.2 6.8 %collective-permute-start = (bf16[256,64]{0,1:T(8,128)(2,1)S(1)}, bf16[256,64]{0,1:T(8,128)(2,1)S(1)}, u32[]{:S(2)}, u32[]{:S(2)}) collective-permute-start(bf16[256,64]{0,1:T(8,128)(2,1)S(1)} %convolution_convert_fusion.4), channel_id=1, source_target_pairs={{0,1},{1,0},{2,3},{3,2},{4,5},{5,4},{6,7},{7,6},{8,9},{9,8},{10,11... | collective-permute-start | bytes 98312 | tf_op jit(solution)/shard_map/ppermute | solution.py:16
  86.9 76.8 %copy-start.1 = (bf16[1,16,8192]{2,1,0:T(8,128)(2,1)S(1)}, bf16[1,16,8192]{2,1,0:T(8,128)(2,1)}, u32[]{:S(2)}) copy-start(bf16[1,16,8192]{2,1,0:T(8,128)(2,1)} %param.8) | copy-start | bytes 786436
  86.9 175.3 %all-gather.6.cloned.1.call-start = ((), (), s32[]{:S(2)}) async-start(), calls=%async_computation.9 | async-start | bytes 8912896 | tf_op jit(solution)/shard_map/all_gather | solution.py:166
  164.7 52.5 %copy-start.4 = (bf16[1,16,8192]{2,1,0:T(8,128)(2,1)}, bf16[1,16,8192]{2,1,0:T(8,128)(2,1)S(1)}, u32[]{:S(2)}) copy-start(bf16[1,16,8192]{2,1,0:T(8,128)(2,1)S(1)} %fusion.26) | copy-start | bytes 786436
  172.0 58.1 %copy-start.5 = (bf16[1,16,4096]{2,1,0:T(8,128)(2,1)S(1)}, bf16[1,16,4096]{2,1,0:T(8,128)(2,1)}, u32[]{:S(2)}) copy-start(bf16[1,16,4096]{2,1,0:T(8,128)(2,1)} %param.14) | copy-start | bytes 393220
  231.2 31.0 %all-to-all-start = ((bf16[8,1,16,4096]{3,2,1,0:T(8,128)(2,1)}), bf16[8,1,16,4096]{3,2,1,0:T(8,128)(2,1)S(1)}, u32[]{:S(2)}, u32[]{:S(2)}) async-start(bf16[8,1,16,4096]{3,2,1,0:T(8,128)(2,1)} %broadcast_in_dim.41), calls=%async_computation.1 | async-start | bytes 2097152 | tf_op jit(solution)/shard_map/all_to_all | solution.py:21
  234.7 128.8 %all-gather.8.cloned.1.call-start = ((), (), s32[]{:S(2)}) async-start(), calls=%async_computation.10 | async-start | bytes 4456448 | tf_op jit(solution)/shard_map/all_gather | solution.py:192
  285.7 49.1 %copy-start.2 = (bf16[128,1024]{1,0:T(8,128)(2,1)S(1)}, bf16[128,1024]{1,0:T(8,128)(2,1)}, u32[]{:S(2)}) copy-start(bf16[128,1024]{1,0:T(8,128)(2,1)} %fusion.23) | copy-start | bytes 786436
  329.1 12.9 %all-to-all-start.3 = ((f32[16,1,1]{2,1,0:T(1,128)}), f32[16,1,1]{2,1,0:T(1,128)S(1)}, u32[]{:S(2)}, u32[]{:S(2)}) async-start(f32[16,1,1]{2,1,0:T(1,128)} %broadcast_in_dim.43), calls=%async_computation.4 | async-start | bytes 16384 | tf_op jit(solution)/shard_map/all_to_all | solution.py:21
  342.0 20.7 %all-to-all-start.4 = ((bf16[8,16,4096]{2,1,0:T(8,128)(2,1)}), bf16[8,16,4096]{2,1,0:T(8,128)(2,1)S(1)}, u32[]{:S(2)}, u32[]{:S(2)}) async-start(bf16[8,16,4096]{2,1,0:T(8,128)(2,1)} %bitcast.25), calls=%async_computation.5 | async-start | bytes 2097152 | tf_op jit(solution)/shard_map/all_to_all | solution.py:56
Sparse Core Ops, SparseCore 0:
  11.0 58.3 all-gather.3
  87.0 76.6 reduce-scatter.1
  166.2 73.9 all-gather.5
  278.5 63.0 all-gather.7
where the time goes:
time: 377 us; the launch traced here: 376 us
  waiting for transfers between devices  135 us (36%)
  other arithmetic  72 us (19%)
  local copies, waits for them, and re-layouts  54.7 us (15%)
  blocking collectives  52.1 us (14%)
  matrix products  32 us (8%)
  between operations  16.4 us (4%)
  starting transfers between devices  13.8 us (4%)
    reduce_scatter x1, waiting for transfers between devices, shards(): lax.psum_scatter(round_bf16(jnp.dot(block, out_local, preferred_element_t...  76.1 us
    all_gather x1, waiting for transfers between devices, shards(): block_rows = lax.all_gather(normed, 'tp', axis=0, tiled=True)  58.2 us
    unnamed x2, other arithmetic  45.3 us
    all_to_all x1, blocking collectives, shards(): lax.all_to_all(gathered, 'tp', split_axis=2, concat_axis=1, tiled=True)  31.7 us
    unnamed x22, local copies, waits for them, and re-layouts  27.2 us
    all_to_all x1, blocking collectives, shards(): lax.all_to_all(teacher_next[None], 'section', split_axis=2, concat_axis=0...  10.6 us
    all_to_all x1, blocking collectives, from_everyone(): return lax.all_to_all(copies, axis, split_axis=0, concat_axis=0, tiled=True)  9.85 us
    all_to_all x2, starting transfers between devices, from_everyone(): return lax.all_to_all(copies, axis, split_axis=0, concat_axis=0, tiled=True)  9.24 us
  transfers between devices with their start and end apart: 9, of which 2 were waited for; matrix products, arithmetic and copies ran while one was open for 36% of the time, Pallas kernels for 0%

commit v1 on v0

--- a/solution.py
+++ b/solution.py
@@ -184,7 +184,10 @@
         "section",
         0,
     )
-    by_column = lax.all_to_all(gathered, "tp", split_axis=2, concat_axis=1, tiled=True)
+    by_column = jnp.concatenate(
+        lax.all_to_all(jnp.stack(jnp.split(gathered, lax.axis_size("tp"), 2), axis=0), "tp", 0, 0),
+        1,
+    )
     slope_stacked = slope.reshape(gathered.shape[0], gathered.shape[1], slope.shape[1])
     block = by_column
     grad_proj = lax.dot_general(

time: 377 us -> 357 us (0.947)
  local copies, waits for them, and re-layouts: 54.7 us -> 20.1 us
  waiting for transfers between devices: 135 us -> 150 us
    unnamed x22 -> x34, local copies, waits for them, and re-layouts: 27.2 us -> 8.03 us
    all_to_all x1, waiting for transfers between devices: 0.01 us -> 15.4 us  [sent_and_summed(): lax.all_to_all(pieces, axis, split_axis=0, concat_axis=0, tiled=True)]
    all_to_all x1 -> x0, local copies, waits for them, and re-layouts: 8.27 us -> none  [shards(): lax.all_to_all(gathered, 'tp', split_axis=2, concat_axis=1, tiled=True)]
    reshape x1, local copies, waits for them, and re-layouts: 7.32 us -> 0.09 us  [shards(): jnp.concatenate(lax.all_to_all(jnp.stack(jnp.split(gathered, lax.axis_siz...]
  transfers between devices with their start and end apart: 9 -> 9, of which waited for: 2 -> 3; matrix products, arithmetic and copies ran while one was open for 36% -> 29% of each run, Pallas kernels for 0% -> 0%
where the time goes in v1:
time: 357 us; the launch traced here: 356 us
  waiting for transfers between devices  150 us (42%)
  other arithmetic  72 us (20%)
  blocking collectives  50.1 us (14%)
  matrix products  33.5 us (9%)
  local copies, waits for them, and re-layouts  20.1 us (6%)
  between operations  16.5 us (5%)
  starting transfers between devices  13.2 us (4%)
    reduce_scatter x1, waiting for transfers between devices, shards(): lax.psum_scatter(round_bf16(jnp.dot(block, out_local, preferred_element_t...  76.1 us
    all_gather x1, waiting for transfers between devices, shards(): block_rows = lax.all_gather(normed, 'tp', axis=0, tiled=True)  58.2 us
    unnamed x2, other arithmetic  45.3 us
    all_to_all x1, blocking collectives, shards(): lax.all_to_all(jnp.stack(jnp.split(gathered, lax.axis_size('tp'), 2), axi...  29.6 us
    all_to_all x1, waiting for transfers between devices, sent_and_summed(): lax.all_to_all(pieces, axis, split_axis=0, concat_axis=0, tiled=True)  15.4 us
    all_to_all x1, blocking collectives, shards(): lax.all_to_all(teacher_next[None], 'section', split_axis=2, concat_axis=0...  10.6 us
    all_to_all x1, blocking collectives, from_everyone(): return lax.all_to_all(copies, axis, split_axis=0, concat_axis=0, tiled=True)  9.85 us
    all_to_all x2, starting transfers between devices, from_everyone(): return lax.all_to_all(copies, axis, split_axis=0, concat_axis=0, tiled=True)  8.58 us
  transfers between devices with their start and end apart: 9, of which 3 were waited for; matrix products, arithmetic and copies ran while one was open for 29% of the time, Pallas kernels for 0%

profile of v1, /device:TPU:1, one launch (start us, length us, event | category | flops | bytes accessed | tf_op | source)
XLA Modules:
  0.0 355.6 jit_solution(1296914501224784408)
XLA Ops:
  7.2 0.0 all-gather.4.cloned.1.call-start
  7.2 1.3 fusion.16
  8.5 1.8 fusion.18
  10.3 0.0 reduce-scatter.2.cloned.1.call-start
  11.0 0.1 fusion.29
  11.2 58.2 %all-gather.4.cloned.1.call-done = bf16[256,8192]{1,0:T(8,128)(2,1)} async-done(((bf16[16,8192]{1,0:T(8,128)(2,1)}), bf16[256,8192]{1,0:T(8,128)(2,1)}) %all-gather.4.cloned.1.call-update) | async-done | bytes 4194320 | tf_op jit(solution)/shard_map/all_gather | solution.py:129
  69.4 4.0 %convolution_convert_fusion.3 = bf16[256,64]{0,1:T(8,128)(2,1)S(1)} fusion(bf16[256,8192]{1,0:T(8,128)(2,1)} %all-gather.4.cloned.1.call-done, bf16[1,2,8192,64]{2,3,1,0:T(8,128)(2,1)} %param.11), kind=kOutput, calls=%fused_computation.13 | convolution fusion | flops 268451840 | bytes 5275648 | tf_op jit(solution)/shard_map/dot_general | solution.py:133
  73.4 0.3 collective-permute-start.1
  73.8 1.4 convolution_convert_fusion.4
  75.2 0.3 collective-permute-start
  75.5 5.8 %fusion.8 = bf16[32,4,8,128]{3,2,1,0:T(8,128)(2,1)S(1)} fusion(bf16[256,8192]{1,0:T(8,128)(2,1)S(1)} %copy-done, bf16[1,8192,512]{2,1,0:T(8,128)(2,1)} %param.10), kind=kOutput, calls=%fused_computation.12 | convolution fusion | flops 2147614720 | bytes 12845056 | tf_op jit(solution)/shard_map/dot_general | solution.py:130
  81.4 0.4 fusion.66
  81.7 0.2 fusion.15
  81.9 0.4 convolution_convert_fusion.2
  82.4 4.5 %convolution_convert_fusion = bf16[256,8192]{1,0:T(8,128)(2,1)} fusion(bf16[256,512]{0,1:T(8,128)(2,1)S(1)} %bitcast.186, bf16[1,512,8192]{2,1,0:T(8,128)(2,1)S(1)} %bitcast.181), kind=kOutput, calls=%fused_computation | convolution fusion | flops 2149580800 | bytes 12845056 | tf_op jit(solution)/shard_map/dot_general | solution.py:151
  86.9 0.2 all-gather.6.cloned.1.call-start
  87.1 0.5 all-gather.6.cloned.1.call-update
  87.6 76.1 %reduce-scatter.2.cloned.1.call-done = bf16[16,8192]{1,0:T(8,128)(2,1)} async-done(((bf16[256,8192]{1,0:T(8,128)(2,1)}), bf16[16,8192]{1,0:T(8,128)(2,1)}) %reduce-scatter.2.cloned.1.call-update) | async-done | bytes 262160 | tf_op jit(solution)/shard_map/reduce_scatter | solution.py:150
  163.7 1.0 fusion.26
  164.7 6.8 %copy.59 = bf16[1,16,8192]{1,0,2:T(2,128)(2,1)} copy(bf16[1,16,8192]{2,1,0:T(8,128)(2,1)S(1)} %fusion.26) | data formatting | bytes 524288 | tf_op jit(solution)/shard_map/broadcast_in_dim | solution.py:199
  171.5 0.5 broadcast.68
  172.0 45.2 %reduce.8 = bf16[8192,16]{1,0:T(8,128)(2,1)S(1)} reduce(bf16[8192,1,16]{2,1,0:T(2,128)(2,1)} %bitcast.161, bf16[]{:T(256)} %broadcast.68), dimensions={1}, to_apply=%bitcast.141.reduce_sub_computation | reduce | bytes 524290
  217.3 2.2 reshape.131
  219.5 10.6 %all_to_all.36 = bf16[8,2,8192]{2,1,0:T(2,128)(2,1)S(1)} all-to-all(bf16[8,2,8192]{2,1,0:T(2,128)(2,1)S(1)} %reshape.131), channel_id=1, replica_groups=mesh['section'=8,'tp'=16] {'section'}, dimensions={0} | all-to-all | bytes 524288 | tf_op jit(solution)/shard_map/all_to_all | solution.py:164
  230.1 1.1 broadcast_in_dim.41
  231.2 3.6 %all-to-all-start = ((bf16[8,1,16,4096]{3,2,1,0:T(8,128)(2,1)}), bf16[8,1,16,4096]{3,2,1,0:T(8,128)(2,1)S(1)}, u32[]{:S(2)}, u32[]{:S(2)}) async-start(bf16[8,1,16,4096]{3,2,1,0:T(8,128)(2,1)} %broadcast_in_dim.41), calls=%async_computation.1 | async-start | bytes 2097152 | tf_op jit(solution)/shard_map/all_to_all | solution.py:21
  234.7 0.0 all-gather.8.cloned.1.call-start
  234.8 5.1 %reshape.132 = bf16[8192,1,16]{2,1,0:T(2,128)(2,1)} reshape(bf16[8,2,8192]{2,1,0:T(2,128)(2,1)S(1)} %all_to_all.36) | data formatting | bytes 524288
  239.9 8.5 %convert_multiply_fusion.2 = f32[1,16,8192]{1,0,2:T(1,128)} fusion(bf16[8192,1,16]{2,1,0:T(2,128)(2,1)} %reshape.132), kind=kLoop, calls=%fused_computation.100 | loop fusion | flops 262144 | bytes 786432 | tf_op jit(solution)/shard_map/mul | solution.py:172
  248.4 2.5 reduce_sum.89
  250.8 0.1 reduce_sum.91
  250.9 8.5 %bitcast_convert_fusion = f32[1,16,8192]{1,0,2:T(1,128)} fusion(bf16[8192,1,16]{2,1,0:T(2,128)(2,1)} %reshape.132), kind=kLoop, calls=%fused_computation.104 | loop fusion | flops 131072 | bytes 786432 | tf_op jit(solution)/shard_map/convert_element_type | solution.py:165
  259.4 2.8 copy.60
  262.2 0.0 all-gather.6.cloned.1.call-done
  262.2 4.7 %fusion.20 = (f32[128]{0:T(128)S(1)}, f32[128]{0:T(128)S(1)}, f32[128,1024]{1,0:T(8,128)S(1)}) fusion(f32[1,16,8,1024]{3,1,2,0:T(8,128)S(1)} %copy.60, bf16[128,4096]{1,0:T(8,128)(2,1)S(1)} %bitcast.163, bf16[4096,1024]{1,0:T(8,128)(2,1)} %all-gather.6.cloned.1.call-done), kind=kOutput, calls=%fused_computation.31 | convolution fusion | flops 1074265856 | bytes 10486784 | tf_op jit(solution)/shard_map/dot_general | solution.py:167
  267.0 9.9 %all_to_all.37 = f32[8,1,384]{2,1,0:T(1,128)S(1)} all-to-all(f32[8,1,384]{2,1,0:T(1,128)S(1)} %broadcast_in_dim.42), channel_id=1, replica_groups=mesh['section'=8,'tp'=16] {'section'}, dimensions={0} | all-to-all | bytes 24576 | tf_op jit(solution)/shard_map/all_to_all | solution.py:21
  276.9 0.6 multiply_multiply_fusion
  277.5 0.9 fusion.23
  278.7 29.6 %all_to_all.38 = bf16[16,8,16,256]{3,2,1,0:T(8,128)(2,1)S(1)} all-to-all(bf16[16,8,16,256]{3,2,1,0:T(8,128)(2,1)S(1)} %fusion.30), channel_id=1, replica_groups=mesh['section'=8,'tp'=16] {'tp'}, dimensions={0} | all-to-all | bytes 2097152 | tf_op jit(solution)/shard_map/all_to_all | solution.py:188
  308.3 1.2 broadcast_in_dim.43
  309.5 5.0 %all-to-all-start.3 = ((f32[16,1,1]{2,1,0:T(1,128)}), f32[16,1,1]{2,1,0:T(1,128)S(1)}, u32[]{:S(2)}, u32[]{:S(2)}) async-start(f32[16,1,1]{2,1,0:T(1,128)} %broadcast_in_dim.43), calls=%async_computation.4 | async-start | bytes 16384 | tf_op jit(solution)/shard_map/all_to_all | solution.py:21
  314.5 7.8 %convolution_convert_fusion.1 = bf16[128,4096]{1,0:T(8,128)(2,1)} fusion(bf16[128,1024]{1,0:T(8,128)(2,1)S(1)} %copy-done.2, bf16[4096,1024]{1,0:T(8,128)(2,1)} %all-gather.6.cloned.1.call-done), kind=kOutput, calls=%fused_computation.4 | convolution fusion | flops 1074266112 | bytes 9699328 | tf_op jit(solution)/shard_map/dot_general | solution.py:181
  322.3 3.6 %all-to-all-start.4 = ((bf16[8,16,4096]{2,1,0:T(8,128)(2,1)}), bf16[8,16,4096]{2,1,0:T(8,128)(2,1)S(1)}, u32[]{:S(2)}, u32[]{:S(2)}) async-start(bf16[8,16,4096]{2,1,0:T(8,128)(2,1)} %bitcast.25), calls=%async_computation.5 | async-start | bytes 2097152 | tf_op jit(solution)/shard_map/all_to_all | solution.py:56
  325.9 0.1 copy.65
  326.0 0.6 reduce_sum.94
  327.2 15.4 %all-to-all-done.4 = bf16[8,16,4096]{2,1,0:T(8,128)(2,1)S(1)} async-done(((bf16[8,16,4096]{2,1,0:T(8,128)(2,1)}), bf16[8,16,4096]{2,1,0:T(8,128)(2,1)S(1)}, u32[]{:S(2)}, u32[]{:S(2)}) %all-to-all-start.4) | async-done | bytes 1048608 | tf_op jit(solution)/shard_map/all_to_all | solution.py:56
  342.7 0.8 convert_reduce_fusion
  343.5 4.4 %convolution_bitcast_fusion = f32[256,1024]{1,0:T(8,128)} fusion(bf16[8,256,256]{2,1,0:T(8,128)(2,1)S(1)} %bitcast.182, bf16[8,256,1024]{2,1,0:T(8,128)(2,1)} %all-gather.8.cloned.1.call-done), kind=kOutput, calls=%fused_computation.6 | convolution fusion | flops 1073741824 | bytes 6291456 | tf_op jit(solution)/shard_map/dot_general | solution.py:193
  (46 shorter events, 0.3 us)
Async XLA Ops:
  7.2 66.6 %copy-start.3 = (bf16[1,2,8192,64]{2,3,1,0:T(8,128)(2,1)S(1)}, bf16[1,2,8192,64]{2,3,1,0:T(8,128)(2,1)}, u32[]{:S(2)}) copy-start(bf16[1,2,8192,64]{2,3,1,0:T(8,128)(2,1)} %param.11) | copy-start | bytes 6291460
  7.2 62.2 %all-gather.4.cloned.1.call-start = ((), (), s32[]{:S(2)}) async-start(), calls=%async_computation.7 | async-start | bytes 4456448 | tf_op jit(solution)/shard_map/all_gather | solution.py:129
  10.3 153.4 %reduce-scatter.2.cloned.1.call-start = ((), (), s32[]{:S(2)}) async-start(), calls=%async_computation.8 | async-start | bytes 4456448 | tf_op jit(solution)/shard_map/reduce_scatter | solution.py:150
  69.4 4.4 %copy-start = (bf16[256,8192]{1,0:T(8,128)(2,1)S(1)}, bf16[256,8192]{1,0:T(8,128)(2,1)}, u32[]{:S(2)}) copy-start(bf16[256,8192]{1,0:T(8,128)(2,1)} %all-gather.4.cloned.1.call-done) | copy-start | bytes 12582916
  73.4 7.9 %collective-permute-start.1 = (bf16[256,64]{0,1:T(8,128)(2,1)S(1)}, bf16[256,64]{0,1:T(8,128)(2,1)S(1)}, u32[]{:S(2)}, u32[]{:S(2)}) collective-permute-start(bf16[256,64]{0,1:T(8,128)(2,1)S(1)} %convolution_convert_fusion.3), channel_id=1, source_target_pairs={{0,1},{1,0},{2,3},{3,2},{4,5},{5,4},{6,7},{7,6},{8,9},{9,8},{10,11... | collective-permute-start | bytes 98312 | tf_op jit(solution)/shard_map/ppermute | solution.py:16
  73.8 8.6 %slice-start = ((s8[8388608]{0:T(1024)(128)(4,1)}), s8[4194304]{0:T(1024)(128)(4,1)S(1)}, s32[]{:S(2)}) async-start(s8[8388608]{0:T(1024)(128)(4,1)} %bitcast.180), calls=%async_computation.11 | async-start | bytes 8388608
  75.2 7.2 %slice-start.1 = ((s8[8388608]{0:T(1024)(128)(4,1)}), s8[4194304]{0:T(1024)(128)(4,1)S(1)}, s32[]{:S(2)}) async-start(s8[8388608]{0:T(1024)(128)(4,1)} %bitcast.180), calls=%async_computation.12 | async-start | bytes 8388608
  75.2 6.8 %collective-permute-start = (bf16[256,64]{0,1:T(8,128)(2,1)S(1)}, bf16[256,64]{0,1:T(8,128)(2,1)S(1)}, u32[]{:S(2)}, u32[]{:S(2)}) collective-permute-start(bf16[256,64]{0,1:T(8,128)(2,1)S(1)} %convolution_convert_fusion.4), channel_id=1, source_target_pairs={{0,1},{1,0},{2,3},{3,2},{4,5},{5,4},{6,7},{7,6},{8,9},{9,8},{10,11... | collective-permute-start | bytes 98312 | tf_op jit(solution)/shard_map/ppermute | solution.py:16
  86.9 76.8 %copy-start.1 = (bf16[1,16,8192]{2,1,0:T(8,128)(2,1)S(1)}, bf16[1,16,8192]{2,1,0:T(8,128)(2,1)}, u32[]{:S(2)}) copy-start(bf16[1,16,8192]{2,1,0:T(8,128)(2,1)} %param.8) | copy-start | bytes 786436
  86.9 175.3 %all-gather.6.cloned.1.call-start = ((), (), s32[]{:S(2)}) async-start(), calls=%async_computation.9 | async-start | bytes 8912896 | tf_op jit(solution)/shard_map/all_gather | solution.py:166
  164.7 6.8 %copy-start.4 = (bf16[1,16,8192]{2,1,0:T(8,128)(2,1)}, bf16[1,16,8192]{2,1,0:T(8,128)(2,1)S(1)}, u32[]{:S(2)}) copy-start(bf16[1,16,8192]{2,1,0:T(8,128)(2,1)S(1)} %fusion.26) | copy-start | bytes 786436
  172.0 58.1 %copy-start.5 = (bf16[1,16,4096]{2,1,0:T(8,128)(2,1)S(1)}, bf16[1,16,4096]{2,1,0:T(8,128)(2,1)}, u32[]{:S(2)}) copy-start(bf16[1,16,4096]{2,1,0:T(8,128)(2,1)} %param.14) | copy-start | bytes 393220
  231.2 31.0 %all-to-all-start = ((bf16[8,1,16,4096]{3,2,1,0:T(8,128)(2,1)}), bf16[8,1,16,4096]{3,2,1,0:T(8,128)(2,1)S(1)}, u32[]{:S(2)}, u32[]{:S(2)}) async-start(bf16[8,1,16,4096]{3,2,1,0:T(8,128)(2,1)} %broadcast_in_dim.41), calls=%async_computation.1 | async-start | bytes 2097152 | tf_op jit(solution)/shard_map/all_to_all | solution.py:21
  234.7 108.8 %all-gather.8.cloned.1.call-start = ((), (), s32[]{:S(2)}) async-start(), calls=%async_computation.10 | async-start | bytes 4456448 | tf_op jit(solution)/shard_map/all_gather | solution.py:195
  278.3 36.2 %copy-start.2 = (bf16[128,1024]{1,0:T(8,128)(2,1)S(1)}, bf16[128,1024]{1,0:T(8,128)(2,1)}, u32[]{:S(2)}) copy-start(bf16[128,1024]{1,0:T(8,128)(2,1)} %fusion.23) | copy-start | bytes 786436
  309.5 12.8 %all-to-all-start.3 = ((f32[16,1,1]{2,1,0:T(1,128)}), f32[16,1,1]{2,1,0:T(1,128)S(1)}, u32[]{:S(2)}, u32[]{:S(2)}) async-start(f32[16,1,1]{2,1,0:T(1,128)} %broadcast_in_dim.43), calls=%async_computation.4 | async-start | bytes 16384 | tf_op jit(solution)/shard_map/all_to_all | solution.py:21
  322.3 20.4 %all-to-all-start.4 = ((bf16[8,16,4096]{2,1,0:T(8,128)(2,1)}), bf16[8,16,4096]{2,1,0:T(8,128)(2,1)S(1)}, u32[]{:S(2)}, u32[]{:S(2)}) async-start(bf16[8,16,4096]{2,1,0:T(8,128)(2,1)} %bitcast.25), calls=%async_computation.5 | async-start | bytes 2097152 | tf_op jit(solution)/shard_map/all_to_all | solution.py:56
Sparse Core Ops, SparseCore 0:
  11.0 58.3 all-gather.3
  87.0 76.6 reduce-scatter.1
  166.2 73.9 all-gather.5
  278.5 60.6 all-gather.7
